TPU v7x, 32 devices: a whole 2x2x4 slice. The times are simulated.
32 devices in a mesh: group: 2 (over y), row: 4 (over z), col: 2 (over x), sub: 2 (over core).
Axes of the slice: x: 2, y: 2, z: 4, core: 2. Of those that a mesh axis runs over, the one named last changes fastest.
Arguments:
- anomalies: bfloat16 [2048, 2048], P(('group', 'row', 'sub')), parts along dimension 0, may hold values from -6 to 6
- innovations: float32 [4096], P(('group', 'row', 'col', 'sub')), parts along dimension 0, may hold values from -12 to 12
- obs_error: float32 [4096], P(('group', 'row', 'col', 'sub')), parts along dimension 0, may hold values from 0.5 to 2
- track_pos: float32 [4096], P('group'), parts along dimension 0, may hold values from 0 to 1
- taper_class: int32 [8, 4], P('group'), parts along dimension 0, may hold values from 0 to 3, as said below
Outputs:
- solution: float32 [4096], P(('group', 'row', 'col', 'sub')), parts along dimension 0
- residual: float32 [4096], P(('group', 'row', 'col', 'sub')), parts along dimension 0
There are 2 independent parts, one for each index of `group`. A program takes and returns all parts, laid end to end along the dimension named above; each array names one. Nothing has to cross between parts.
Inputs may be any that keep to these rules, and one draw needn't show every extreme that they name: `taper_class`: tiles are spatial blocks of the region, laid along the plume in an order given by a permutation pos of the 4 tiles; entry (a, b) is the distance |pos[a] - pos[b]| in tiles.
All inputs are finite; a program needn't handle non-finite values.
Results may differ from a plain program's by a relative error of at most 0.0003.
Values may be sent and summed in bfloat16 or wider, within the bound.
No kernel may reach another device: no remote copies, remote signals or barrier semaphores. Data moves between devices by JAX's collectives and lax.ppermute only.
A program may use at most 64 MiB of HBM per device.

v0:
```python
import jax
import jax.numpy as jnp
from jax import lax
from jax.sharding import PartitionSpec as P

ITERS = 2
track_width = 0.0001


def squares(residual):
    return lax.psum(jnp.sum(residual * residual), ("row", "col", "sub"))


def per_device(anomalies, innovations, obs_error, track_pos, taper_class):
    row_count = lax.axis_size("row")
    col_count = lax.axis_size("col")
    sub_count = lax.axis_size("sub")
    row_index = lax.axis_index("row")
    col_index = lax.axis_index("col")
    local_members, total_obs = anomalies.shape
    block_len = total_obs // row_count
    quarter_len = block_len // col_count
    member_total = local_members * row_count * sub_count
    inverse_members = 1.0 / (member_total - 1)
    reach_tiles = max(2, row_count // 4)
    class_row = lax.dynamic_index_in_dim(taper_class, row_index, 0, keepdims=False)
    tile_weight = jnp.maximum(0.0, 1.0 - class_row.astype(jnp.float32) / reach_tiles)
    row_pos = lax.dynamic_slice_in_dim(track_pos, row_index * block_len, block_len, 0)
    col_pos = lax.dynamic_index_in_dim(
        track_pos.reshape(row_count, col_count, quarter_len), col_index, 1, keepdims=False
    )
    own_block = lax.all_to_all(anomalies, "row", split_axis=1, concat_axis=0, tiled=True)
    own_quarter = lax.dynamic_slice_in_dim(own_block, col_index * quarter_len, quarter_len, 1)

    def one_tile(piece, block_index, keep_factor):
        product = jnp.einsum("mi,mq->iq", own_block, piece, preferred_element_type=jnp.float32)
        column_pos = lax.dynamic_index_in_dim(col_pos, block_index, 0, keepdims=False)
        weight_here = lax.dynamic_index_in_dim(tile_weight, block_index, 0, keepdims=False)
        distance = row_pos[:, None] - column_pos[None, :]
        taper = weight_here * keep_factor * jnp.exp(-(distance * distance) / track_width)
        return product * (taper * inverse_members)

    def one_entry(entry):
        return one_tile(entry[0], entry[1], 1.0)

    piece = lax.all_gather(own_quarter[None], "row", axis=0, tiled=True)
    indices = jnp.arange(piece.shape[0], dtype=jnp.int32)
    tiles = lax.map(one_entry, (piece, indices))
    solution = jnp.zeros_like(innovations)
    residual = innovations
    direction_vec = innovations
    norm_now = squares(residual)
    for turn_index in range(ITERS):
        column_vec = lax.all_gather(direction_vec, ("row", "sub"), axis=0, tiled=True).reshape(
            row_count, quarter_len
        )
        direct = jnp.einsum("jiq,jq->i", tiles, column_vec, precision=lax.Precision.HIGHEST)
        extra = obs_error * direction_vec
        own_part = lax.psum_scatter(direct, ("col", "sub"), scatter_dimension=0, tiled=True)
        image = own_part + extra
        alpha = norm_now / lax.psum(jnp.sum(direction_vec * image), ("row", "col", "sub"))
        solution = solution + alpha * direction_vec
        residual = residual - alpha * image
        if turn_index + 1 < ITERS:
            norm_next = squares(residual)
            direction_vec = residual + norm_next / norm_now * direction_vec
            norm_now = norm_next
    return (solution, residual)


def solution(mesh):
    in_specs = (
        P(("group", "row", "sub"), None),
        P(("group", "row", "col", "sub")),
        P(("group", "row", "col", "sub")),
        P("group"),
        P("group", None),
    )
    out_specs = (P(("group", "row", "col", "sub")), P(("group", "row", "col", "sub")))
    return jax.shard_map(
        per_device, mesh=mesh, in_specs=in_specs, out_specs=out_specs, check_vma=False
    )
```

profile of v0, /device:TPU:0, one launch (start us, length us, event | category | flops | bytes accessed | tf_op | source)
XLA Modules:
  0.0 207.6 jit_solution(16276653144272945120)
XLA Ops:
  7.2 0.0 copy-start.3
  7.2 0.0 copy-start
  7.2 0.0 copy-start.1
  7.2 1.9 copy.16
  9.1 6.3 %all-to-all-start = ((bf16[128,4,512]{2,0,1:T(8,128)(2,1)}), bf16[128,4,512]{2,0,1:T(8,128)(2,1)S(1)}, u32[]{:S(2)}, u32[]{:S(2)}) async-start(bf16[128,4,512]{2,0,1:T(8,128)(2,1)} %bitcast.41), calls=%async_computation | async-start | bytes 1048576 | tf_op jit(solution)/shard_map/all_to_all | solution.py:32
  15.4 0.0 all-gather.5.cloned.1.call-start
  15.4 14.5 %all-to-all-done = bf16[128,4,512]{2,0,1:T(8,128)(2,1)S(1)} async-done(((bf16[128,4,512]{2,0,1:T(8,128)(2,1)}), bf16[128,4,512]{2,0,1:T(8,128)(2,1)S(1)}, u32[]{:S(2)}, u32[]{:S(2)}) %all-to-all-start) | async-done | bytes 524320 | tf_op jit(solution)/shard_map/all_to_all | solution.py:32
  29.9 0.7 constant_dynamic-slice_fusion.3
  30.6 0.0 all-gather.5.cloned.1.call-update
  30.7 0.0 copy-done
  30.7 0.1 dynamic_slice.32
  30.8 0.0 copy-done.3
  30.8 0.6 dynamic-slice
  32.0 0.0 copy-done.1
  32.1 9.8 %all-gather.1 = f32[8,1,128]{2,1,0:T(1,128)S(1)} all-gather(f32[1,1,128]{2,1,0:T(1,128)S(1)} %bitcast.64), channel_id=1, replica_groups=mesh['group'=2,'row'=4,'col'=2,'sub'=2] {'row','sub'}, dimensions={0}, use_global_device_ids=true | all-gather | bytes 4608 | tf_op jit(solution)/shard_map/all_gather | solution.py:54
  41.8 0.7 maximum_bitcast_fusion
  42.5 15.3 %all-gather.5.cloned.1.call-done = bf16[2048,256]{1,0:T(8,128)(2,1)} async-done(((bf16[512,256]{1,0:T(8,128)(2,1)}), bf16[2048,256]{1,0:T(8,128)(2,1)}) %all-gather.5.cloned.1.call-update) | async-done | bytes 1048592 | tf_op jit(solution)/shard_map/all_gather | solution.py:46
  57.8 20.4 %while.10 = (s32[]{:T(128)}, f32[4,512,256]{1,2,0:T(8,128)S(1)}, bf16[4,512,256]{2,1,0:T(8,128)(2,1)}, bf16[512,512]{1,0:T(8,128)(2,1)S(1)}, s32[4]{0:T(128)S(1)...) while((s32[]{:T(128)}, f32[4,512,256]{1,2,0:T(8,128)S(1)}, ...), condition=%wide.region_3.4_spmd, body=%wide.region_2.3_spmd.sunk | while | flops 135135232 | bytes 1317547 | solution.py:48
  57.8 0.6 dynamic_slice.56
  60.4 0.6 dynamic_slice.57
  61.0 1.9 fusion.21
  62.9 0.6 dynamic_slice.56
  65.5 0.6 dynamic_slice.57
  66.1 1.9 fusion.21
  68.0 0.6 dynamic_slice.56
  70.6 0.6 dynamic_slice.57
  71.2 1.9 fusion.21
  73.1 0.6 dynamic_slice.56
  75.7 0.6 dynamic_slice.57
  76.3 1.9 fusion.21
  78.2 0.0 copy-start.2
  78.2 1.2 fusion.9
  79.4 6.4 %all-reduce = f32[512]{0:T(512)S(1)} all-reduce(f32[512]{0:T(512)S(1)} %bitcast.66), channel_id=3, replica_groups=mesh['group'=2,'row'=4,'col'=2,'sub'=2] {'col','sub'}, use_global_device_ids=true, to_apply=%region_4.5.clone | all-reduce | flops 512 | bytes 4096
  85.8 0.0 copy-done.2
  85.8 0.7 multiply_reduce_fusion.2
  86.5 31.6 %all-reduce.2 = (f32[]{:T(128)}, f32[]{:T(128)}) all-reduce(f32[]{:T(128)} %get-tuple-element.46, f32[]{:T(128)} %get-tuple-element.45), channel_id=1, replica_groups=mesh['group'=2,'row'=4,'col'=2,'sub'=2] {'row','col','sub'}, use_global_device_ids=true, to_apply=%region_1.2 | all-reduce | flops 2 | bytes 16 | tf_op jit(solution)/shard_map/psum | solution.py:11
  119.5 0.7 multiply_reduce_fusion.1
  120.1 30.1 %psum.30 = f32[]{:T(128)} all-reduce(f32[]{:T(128)} %get-tuple-element.65), channel_id=1, replica_groups=mesh['group'=2,'row'=4,'col'=2,'sub'=2] {'row','col','sub'}, use_global_device_ids=true, to_apply=%region_8.9 | all-reduce | flops 1 | bytes 8 | tf_op jit(solution)/shard_map/psum | solution.py:11
  151.6 8.4 %all-gather.2 = f32[8,1,128]{2,1,0:T(1,128)S(1)} all-gather(f32[1,1,128]{2,1,0:T(1,128)S(1)} %bitcast.67), channel_id=1, replica_groups=mesh['group'=2,'row'=4,'col'=2,'sub'=2] {'row','sub'}, dimensions={0}, use_global_device_ids=true | all-gather | bytes 4608 | tf_op jit(solution)/shard_map/all_gather | solution.py:54
  160.0 1.2 fusion.10
  161.2 5.9 %all-reduce.1 = f32[512]{0:T(512)S(1)} all-reduce(f32[512]{0:T(512)S(1)} %bitcast.65), channel_id=4, replica_groups=mesh['group'=2,'row'=4,'col'=2,'sub'=2] {'col','sub'}, use_global_device_ids=true, to_apply=%region_9.10.clone | all-reduce | flops 512 | bytes 4096
  167.1 0.7 multiply_reduce_fusion
  167.8 31.1 %psum.31 = f32[]{:T(128)} all-reduce(f32[]{:T(128)} %multiply_reduce_fusion), channel_id=1, replica_groups=mesh['group'=2,'row'=4,'col'=2,'sub'=2] {'row','col','sub'}, use_global_device_ids=true, to_apply=%region_11.12 | all-reduce | flops 1 | bytes 8 | tf_op jit(solution)/shard_map/psum | solution.py:61
  200.2 0.6 multiply_subtract_fusion
  (10 shorter events, 0.1 us)
Async XLA Ops:
  7.2 23.6 %copy-start.3 = (u32[32]{0:T(128)S(1)}, u32[32]{0:T(128)}, u32[]{:S(2)}) copy-start(u32[32]{0:T(128)} %constant.61) | copy-start | bytes 388
  7.2 23.5 %copy-start = (f32[2048]{0:T(1024)S(1)}, f32[2048]{0:T(1024)}, u32[]{:S(2)}) copy-start(f32[2048]{0:T(1024)} %param.10) | copy-start | bytes 24580
  7.2 24.9 %copy-start.1 = (f32[128]{0:T(128)S(1)}, f32[128]{0:T(128)}, u32[]{:S(2)}) copy-start(f32[128]{0:T(128)} %param.8) | copy-start | bytes 1540
  9.1 20.8 %all-to-all-start = ((bf16[128,4,512]{2,0,1:T(8,128)(2,1)}), bf16[128,4,512]{2,0,1:T(8,128)(2,1)S(1)}, u32[]{:S(2)}, u32[]{:S(2)}) async-start(bf16[128,4,512]{2,0,1:T(8,128)(2,1)} %bitcast.41), calls=%async_computation | async-start | bytes 1048576 | tf_op jit(solution)/shard_map/all_to_all | solution.py:32
  15.4 42.4 %all-gather.5.cloned.1.call-start = ((), (), s32[]{:S(2)}) async-start(), calls=%async_computation.1 | async-start | bytes 1310720 | tf_op jit(solution)/shard_map/all_gather | solution.py:46
  78.2 7.6 %copy-start.2 = (f32[128]{0:T(128)S(1)}, f32[128]{0:T(128)}, u32[]{:S(2)}) copy-start(f32[128]{0:T(128)} %param.9) | copy-start | bytes 1540
Sparse Core Ops, SparseCore 0:
  30.8 27.0 all-gather.4
where the time goes:
time: 208 us
  blocking collectives  123 us (59%)
  waiting for transfers between devices  29.8 us (14%)
  between operations  18.8 us (9%)
  matrix products  10.1 us (5%)
  local copies, waits for them, and re-layouts  8.07 us (4%)
  loops' own time  7.89 us (4%)
  starting transfers between devices  6.32 us (3%)
  other arithmetic  3.32 us (2%)
    psum x2, blocking collectives, squares(): return lax.psum(jnp.sum(residual * residual), ('row', 'col', 'sub'))  61.7 us
    psum x1, blocking collectives, per_device(): lax.psum(jnp.sum(direction_vec * image), ('row', 'col', 'sub'))  31.1 us
    all_gather x2, blocking collectives, per_device(): lax.all_gather(direction_vec, ('row', 'sub'), axis=0, tiled=True)  18.2 us
    all_gather x1, waiting for transfers between devices, per_device(): piece = lax.all_gather(own_quarter[None], 'row', axis=0, tiled=True)  15.3 us
    all_to_all x1, waiting for transfers between devices, per_device(): lax.all_to_all(anomalies, 'row', split_axis=1, concat_axis=0, tiled=True)  14.5 us
    unnamed x2, blocking collectives  12.3 us
    another operation x1, loops' own time, per_device(): tiles = lax.map(one_entry, (piece, indices))  7.89 us
    dot_general x4, matrix products, one_tile(): jnp.einsum('mi,mq->iq', own_block, piece, preferred_element_type=jnp.floa...  7.74 us
  transfers between devices with their start and end apart: 2, of which 2 were waited for; matrix products, arithmetic and copies ran while one was open for 1% of the time, Pallas kernels for 0%

commit v1 on v0

--- a/solution.py
+++ b/solution.py
@@ -5,6 +5,27 @@
 
 ITERS = 2
 track_width = 0.0001
+
+
+def gather_around(array, axis, dim):
+    size, position, width = (lax.axis_size(axis), lax.axis_index(axis), array.shape[dim])
+    right = [(i, (i + 1) % size) for i in range(size)]
+    backward = [(i, (i - 1) % size) for i in range(size)]
+    result = jnp.zeros((*array.shape[:dim], size * width, *array.shape[dim + 1 :]), array.dtype)
+    result = lax.dynamic_update_slice_in_dim(result, array, position * width, axis=dim)
+    from_left = from_right = array
+    half = size // 2
+    for turn in range(1, half + 1):
+        from_left = lax.ppermute(from_left, axis, right)
+        result = lax.dynamic_update_slice_in_dim(
+            result, from_left, (position - turn) % size * width, axis=dim
+        )
+        if turn < size - half:
+            from_right = lax.ppermute(from_right, axis, backward)
+            result = lax.dynamic_update_slice_in_dim(
+                result, from_right, (position + turn) % size * width, axis=dim
+            )
+    return result
 
 
 def squares(residual):
@@ -51,9 +72,7 @@
     direction_vec = innovations
     norm_now = squares(residual)
     for turn_index in range(ITERS):
-        column_vec = lax.all_gather(direction_vec, ("row", "sub"), axis=0, tiled=True).reshape(
-            row_count, quarter_len
-        )
+        column_vec = gather_around(direction_vec, ("row", "sub"), 0).reshape(row_count, quarter_len)
         direct = jnp.einsum("jiq,jq->i", tiles, column_vec, precision=lax.Precision.HIGHEST)
         extra = obs_error * direction_vec
         own_part = lax.psum_scatter(direct, ("col", "sub"), scatter_dimension=0, tiled=True)

time: 208 us -> 218 us (1.048)
  starting transfers between devices: 6.32 us -> 27.5 us
  blocking collectives: 123 us -> 104 us
  waiting for transfers between devices: 29.8 us -> 34.6 us
  local copies, waits for them, and re-layouts: 8.07 us -> 11.1 us
    ppermute x0 -> x14, starting transfers between devices: none -> 21.2 us  [the longest x6 21.1 us: gather_around(): from_right = lax.ppermute(from_right, axis, backward)]
    all_gather x2 -> x0, blocking collectives: 18.2 us -> none  [per_device(): lax.all_gather(direction_vec, ('row', 'sub'), axis=0, tiled=True)]
    ppermute x0 -> x14, waiting for transfers between devices: none -> 12.2 us  [the longest x8 12.1 us: gather_around(): from_left = lax.ppermute(from_left, axis, right)]
    all_gather x1, waiting for transfers between devices: 15.3 us -> 7.88 us  [per_device(): piece = lax.all_gather(own_quarter[None], 'row', axis=0, tiled=True)]
    dynamic_update_slice x0 -> x15, local copies, waits for them, and re-layouts: none -> 3 us  [the longest x8 1.57 us: gather_around(): lax.dynamic_update_slice_in_dim(result, from_left, (position - turn) % si...]
  transfers between devices with their start and end apart: 2 -> 16, of which waited for: 2 -> 12; matrix products, arithmetic and copies ran while one was open for 1% -> 2% of each run, Pallas kernels for 0% -> 0%
where the time goes in v1:
time: 218 us; the launch traced here: 217 us
  blocking collectives  104 us (48%)
  waiting for transfers between devices  34.6 us (16%)
  starting transfers between devices  27.5 us (13%)
  between operations  18.8 us (9%)
  local copies, waits for them, and re-layouts  11.1 us (5%)
  matrix products  10.1 us (5%)
  loops' own time  7.89 us (4%)
  other arithmetic  3.44 us (2%)
    psum x2, blocking collectives, squares(): return lax.psum(jnp.sum(residual * residual), ('row', 'col', 'sub'))  61.7 us
    psum x1, blocking collectives, per_device(): lax.psum(jnp.sum(direction_vec * image), ('row', 'col', 'sub'))  30.1 us
    ppermute x6, starting transfers between devices, gather_around(): from_right = lax.ppermute(from_right, axis, backward)  21.1 us
    all_to_all x1, waiting for transfers between devices, per_device(): lax.all_to_all(anomalies, 'row', split_axis=1, concat_axis=0, tiled=True)  14.5 us
    unnamed x2, blocking collectives  12.2 us
    ppermute x8, waiting for transfers between devices, gather_around(): from_left = lax.ppermute(from_left, axis, right)  12.1 us
    another operation x1, loops' own time, per_device(): tiles = lax.map(one_entry, (piece, indices))  7.89 us
    all_gather x1, waiting for transfers between devices, per_device(): piece = lax.all_gather(own_quarter[None], 'row', axis=0, tiled=True)  7.88 us
  transfers between devices with their start and end apart: 16, of which 12 were waited for; matrix products, arithmetic and copies ran while one was open for 2% of the time, Pallas kernels for 0%

profile of v1, /device:TPU:0, one launch (start us, length us, event | category | flops | bytes accessed | tf_op | source)
XLA Modules:
  0.0 217.5 jit_solution(3285375980401743923)
XLA Ops:
  7.2 1.9 copy.16
  9.1 6.3 %all-to-all-start = ((bf16[128,4,512]{2,0,1:T(8,128)(2,1)}), bf16[128,4,512]{2,0,1:T(8,128)(2,1)S(1)}, u32[]{:S(2)}, u32[]{:S(2)}) async-start(bf16[128,4,512]{2,0,1:T(8,128)(2,1)} %bitcast.39), calls=%async_computation | async-start | bytes 1048576 | tf_op jit(solution)/shard_map/all_to_all | solution.py:53
  15.4 14.5 %all-to-all-done = bf16[128,4,512]{2,0,1:T(8,128)(2,1)S(1)} async-done(((bf16[128,4,512]{2,0,1:T(8,128)(2,1)}), bf16[128,4,512]{2,0,1:T(8,128)(2,1)S(1)}, u32[]{:S(2)}, u32[]{:S(2)}) %all-to-all-start) | async-done | bytes 524320 | tf_op jit(solution)/shard_map/all_to_all | solution.py:53
  29.9 0.7 constant_dynamic-slice_fusion.3
  30.7 3.5 %collective-permute-start.1 = (f32[128]{0:T(128)S(1)}, f32[128]{0:T(128)S(1)}, u32[]{:S(2)}, u32[]{:S(2)}) collective-permute-start(f32[128]{0:T(128)S(1)} %copy-done.2), channel_id=1, source_target_pairs={{0,13},{1,0},{4,1},{5,4},{8,5},{9,8},{12,9},{13,12},{2,15},{3,2},{... | collective-permute-start | bytes 1544 | tf_op jit(solution)/shard_map/ppermute | solution.py:24
  34.3 0.7 maximum_bitcast_fusion
  35.0 0.1 dynamic_slice.32
  35.1 0.4 collective-permute-done
  35.5 0.2 dynamic_update_slice.52
  35.7 3.6 %collective-permute-start.3 = (f32[128]{0:T(128)S(1)}, f32[128]{0:T(128)S(1)}, u32[]{:S(2)}, u32[]{:S(2)}) collective-permute-start(f32[128]{0:T(128)S(1)} %collective-permute-done.1), channel_id=1, source_target_pairs={{0,13},{1,0},{4,1},{5,4},{8,5},{9,8},{12,9},{13,12},{2,15},{3,2},{... | collective-permute-start | bytes 1544 | tf_op jit(solution)/shard_map/ppermute | solution.py:24
  39.2 1.0 collective-permute-done.2
  40.3 0.6 dynamic-slice
  40.8 3.5 %collective-permute-start.5 = (f32[128]{0:T(128)S(1)}, f32[128]{0:T(128)S(1)}, u32[]{:S(2)}, u32[]{:S(2)}) collective-permute-start(f32[128]{0:T(128)S(1)} %collective-permute-done.3), channel_id=1, source_target_pairs={{0,13},{1,0},{4,1},{5,4},{8,5},{9,8},{12,9},{13,12},{2,15},{3,2},{... | collective-permute-start | bytes 1544 | tf_op jit(solution)/shard_map/ppermute | solution.py:24
  44.4 0.6 collective-permute-done.4
  45.7 0.2 dynamic_update_slice.53
  45.9 0.2 dynamic_update_slice.54
  46.1 0.2 dynamic_update_slice.55
  46.3 0.2 dynamic_update_slice.56
  46.5 0.2 dynamic_update_slice.57
  46.7 0.2 dynamic_update_slice.58
  46.9 2.8 %collective-permute-done.6 = f32[128]{0:T(128)S(1)} collective-permute-done((f32[128]{0:T(128)S(1)}, f32[128]{0:T(128)S(1)}, u32[]{:S(2)}, u32[]{:S(2)}) %collective-permute-start.6) | collective-permute-done | bytes 544 | tf_op jit(solution)/shard_map/ppermute | solution.py:19
  49.8 0.2 dynamic_update_slice.59
  50.0 7.9 %all-gather.3.cloned.1.call-done = bf16[2048,256]{1,0:T(8,128)(2,1)} async-done(((bf16[512,256]{1,0:T(8,128)(2,1)}), bf16[2048,256]{1,0:T(8,128)(2,1)}) %all-gather.3.cloned.1.call-update) | async-done | bytes 1048592 | tf_op jit(solution)/shard_map/all_gather | solution.py:67
  57.9 20.4 %while.10 = (s32[]{:T(128)}, f32[4,512,256]{1,2,0:T(8,128)S(1)}, bf16[4,512,256]{2,1,0:T(8,128)(2,1)}, bf16[512,512]{1,0:T(8,128)(2,1)S(1)}, s32[4]{0:T(128)S(1)...) while((s32[]{:T(128)}, f32[4,512,256]{1,2,0:T(8,128)S(1)}, ...), condition=%wide.region_3.4_spmd, body=%wide.region_2.3_spmd.sunk | while | flops 135135232 | bytes 1317555 | solution.py:69
  57.9 0.6 dynamic_slice.56
  60.4 0.6 dynamic_slice.57
  61.0 1.9 fusion.22
  62.9 0.6 dynamic_slice.56
  65.5 0.6 dynamic_slice.57
  66.1 1.9 fusion.22
  68.0 0.6 dynamic_slice.56
  70.6 0.6 dynamic_slice.57
  71.2 1.9 fusion.22
  73.1 0.6 dynamic_slice.56
  75.7 0.6 dynamic_slice.57
  76.3 1.9 fusion.22
  78.2 1.2 fusion.10
  79.4 6.4 %all-reduce = f32[512]{0:T(512)S(1)} all-reduce(f32[512]{0:T(512)S(1)} %bitcast.63), channel_id=3, replica_groups=mesh['group'=2,'row'=4,'col'=2,'sub'=2] {'col','sub'}, use_global_device_ids=true, to_apply=%region_4.5.clone | all-reduce | flops 512 | bytes 4096
  85.9 0.7 multiply_reduce_fusion.2
  86.5 31.6 %all-reduce.2 = (f32[]{:T(128)}, f32[]{:T(128)}) all-reduce(f32[]{:T(128)} %get-tuple-element.46, f32[]{:T(128)} %get-tuple-element.45), channel_id=1, replica_groups=mesh['group'=2,'row'=4,'col'=2,'sub'=2] {'row','col','sub'}, use_global_device_ids=true, to_apply=%region_1.2 | all-reduce | flops 2 | bytes 16 | tf_op jit(solution)/shard_map/psum | solution.py:32
  119.5 0.7 multiply_reduce_fusion.1
  120.2 30.1 %psum.30 = f32[]{:T(128)} all-reduce(f32[]{:T(128)} %get-tuple-element.67), channel_id=1, replica_groups=mesh['group'=2,'row'=4,'col'=2,'sub'=2] {'row','col','sub'}, use_global_device_ids=true, to_apply=%region_8.9 | all-reduce | flops 1 | bytes 8 | tf_op jit(solution)/shard_map/psum | solution.py:32
  151.6 0.1 fusion.9
  151.8 3.5 %collective-permute-start.8 = (f32[128]{0:T(128)S(1)}, f32[128]{0:T(128)S(1)}, u32[]{:S(2)}, u32[]{:S(2)}) collective-permute-start(f32[128]{0:T(128)S(1)} %get-tuple-element.66), channel_id=1, source_target_pairs={{0,13},{1,0},{4,1},{5,4},{8,5},{9,8},{12,9},{13,12},{2,15},{3,2},{... | collective-permute-start | bytes 1544 | tf_op jit(solution)/shard_map/ppermute | solution.py:24
  155.3 1.2 collective-permute-done.7
  156.5 0.1 collective-permute-done.8
  156.6 3.5 %collective-permute-start.10 = (f32[128]{0:T(128)S(1)}, f32[128]{0:T(128)S(1)}, u32[]{:S(2)}, u32[]{:S(2)}) collective-permute-start(f32[128]{0:T(128)S(1)} %collective-permute-done.8), channel_id=1, source_target_pairs={{0,13},{1,0},{4,1},{5,4},{8,5},{9,8},{12,9},{13,12},{2,15},{3,2},{... | collective-permute-start | bytes 1544 | tf_op jit(solution)/shard_map/ppermute | solution.py:24
  160.1 1.2 collective-permute-done.9
  161.3 0.1 collective-permute-done.10
  161.4 3.5 %collective-permute-start.12 = (f32[128]{0:T(128)S(1)}, f32[128]{0:T(128)S(1)}, u32[]{:S(2)}, u32[]{:S(2)}) collective-permute-start(f32[128]{0:T(128)S(1)} %collective-permute-done.10), channel_id=1, source_target_pairs={{0,13},{1,0},{4,1},{5,4},{8,5},{9,8},{12,9},{13,12},{2,15},{3,2},{... | collective-permute-start | bytes 1544 | tf_op jit(solution)/shard_map/ppermute | solution.py:24
  164.8 1.2 collective-permute-done.11
  166.1 0.2 dynamic_update_slice.61
  166.2 0.2 dynamic_update_slice.62
  166.4 0.2 dynamic_update_slice.63
  166.6 0.2 dynamic_update_slice.64
  166.8 0.2 dynamic_update_slice.65
  167.0 0.2 dynamic_update_slice.66
  167.3 3.6 %collective-permute-done.13 = f32[128]{0:T(128)S(1)} collective-permute-done((f32[128]{0:T(128)S(1)}, f32[128]{0:T(128)S(1)}, u32[]{:S(2)}, u32[]{:S(2)}) %collective-permute-start.13) | collective-permute-done | bytes 544 | tf_op jit(solution)/shard_map/ppermute | solution.py:19
  170.8 0.2 dynamic_update_slice.67
  171.0 1.2 fusion.11
  172.2 5.7 %all-reduce.1 = f32[512]{0:T(512)S(1)} all-reduce(f32[512]{0:T(512)S(1)} %bitcast.62), channel_id=4, replica_groups=mesh['group'=2,'row'=4,'col'=2,'sub'=2] {'col','sub'}, use_global_device_ids=true, to_apply=%region_9.10.clone | all-reduce | flops 512 | bytes 4096
  177.9 0.7 multiply_reduce_fusion
  178.6 30.1 %psum.31 = f32[]{:T(128)} all-reduce(f32[]{:T(128)} %multiply_reduce_fusion), channel_id=1, replica_groups=mesh['group'=2,'row'=4,'col'=2,'sub'=2] {'row','col','sub'}, use_global_device_ids=true, to_apply=%region_11.12 | all-reduce | flops 1 | bytes 8 | tf_op jit(solution)/shard_map/psum | solution.py:80
  210.0 0.6 multiply_subtract_fusion
  (33 shorter events, 0.2 us)
Async XLA Ops:
  7.2 33.1 %copy-start.3 = (u32[32]{0:T(128)S(1)}, u32[32]{0:T(128)}, u32[]{:S(2)}) copy-start(u32[32]{0:T(128)} %constant.132) | copy-start | bytes 388
  7.2 23.5 %copy-start.2 = (f32[128]{0:T(128)S(1)}, f32[128]{0:T(128)}, u32[]{:S(2)}) copy-start(f32[128]{0:T(128)} %param.8) | copy-start | bytes 1540
  7.2 27.1 %copy-start = (f32[2048]{0:T(1024)S(1)}, f32[2048]{0:T(1024)}, u32[]{:S(2)}) copy-start(f32[2048]{0:T(1024)} %param.10) | copy-start | bytes 24580
  9.1 20.8 %all-to-all-start = ((bf16[128,4,512]{2,0,1:T(8,128)(2,1)}), bf16[128,4,512]{2,0,1:T(8,128)(2,1)S(1)}, u32[]{:S(2)}, u32[]{:S(2)}) async-start(bf16[128,4,512]{2,0,1:T(8,128)(2,1)} %bitcast.39), calls=%async_computation | async-start | bytes 1048576 | tf_op jit(solution)/shard_map/all_to_all | solution.py:53
  15.4 42.4 %all-gather.3.cloned.1.call-start = ((), (), s32[]{:S(2)}) async-start(), calls=%async_computation.1 | async-start | bytes 1310720 | tf_op jit(solution)/shard_map/all_gather | solution.py:67
  30.7 4.8 %collective-permute-start = (f32[128]{0:T(128)S(1)}, f32[128]{0:T(128)S(1)}, u32[]{:S(2)}, u32[]{:S(2)}) collective-permute-start(f32[128]{0:T(128)S(1)} %copy-done.2), channel_id=1, source_target_pairs={{0,1},{1,4},{4,5},{5,8},{8,9},{9,12},{12,13},{13,0},{2,3},{3,6},{6... | collective-permute-start | bytes 1544 | tf_op jit(solution)/shard_map/ppermute | solution.py:19
  30.7 5.0 %collective-permute-start.1 = (f32[128]{0:T(128)S(1)}, f32[128]{0:T(128)S(1)}, u32[]{:S(2)}, u32[]{:S(2)}) collective-permute-start(f32[128]{0:T(128)S(1)} %copy-done.2), channel_id=1, source_target_pairs={{0,13},{1,0},{4,1},{5,4},{8,5},{9,8},{12,9},{13,12},{2,15},{3,2},{... | collective-permute-start | bytes 1544 | tf_op jit(solution)/shard_map/ppermute | solution.py:24
  35.5 4.8 %collective-permute-start.2 = (f32[128]{0:T(128)S(1)}, f32[128]{0:T(128)S(1)}, u32[]{:S(2)}, u32[]{:S(2)}) collective-permute-start(f32[128]{0:T(128)S(1)} %collective-permute-done), channel_id=1, source_target_pairs={{0,1},{1,4},{4,5},{5,8},{8,9},{9,12},{12,13},{13,0},{2,3},{3,6},{6... | collective-permute-start | bytes 1544 | tf_op jit(solution)/shard_map/ppermute | solution.py:19
  35.7 5.2 %collective-permute-start.3 = (f32[128]{0:T(128)S(1)}, f32[128]{0:T(128)S(1)}, u32[]{:S(2)}, u32[]{:S(2)}) collective-permute-start(f32[128]{0:T(128)S(1)} %collective-permute-done.1), channel_id=1, source_target_pairs={{0,13},{1,0},{4,1},{5,4},{8,5},{9,8},{12,9},{13,12},{2,15},{3,2},{... | collective-permute-start | bytes 1544 | tf_op jit(solution)/shard_map/ppermute | solution.py:24
  40.2 4.8 %collective-permute-start.4 = (f32[128]{0:T(128)S(1)}, f32[128]{0:T(128)S(1)}, u32[]{:S(2)}, u32[]{:S(2)}) collective-permute-start(f32[128]{0:T(128)S(1)} %collective-permute-done.2), channel_id=1, source_target_pairs={{0,1},{1,4},{4,5},{5,8},{8,9},{9,12},{12,13},{13,0},{2,3},{3,6},{6... | collective-permute-start | bytes 1544 | tf_op jit(solution)/shard_map/ppermute | solution.py:19
  40.8 5.9 %collective-permute-start.5 = (f32[128]{0:T(128)S(1)}, f32[128]{0:T(128)S(1)}, u32[]{:S(2)}, u32[]{:S(2)}) collective-permute-start(f32[128]{0:T(128)S(1)} %collective-permute-done.3), channel_id=1, source_target_pairs={{0,13},{1,0},{4,1},{5,4},{8,5},{9,8},{12,9},{13,12},{2,15},{3,2},{... | collective-permute-start | bytes 1544 | tf_op jit(solution)/shard_map/ppermute | solution.py:24
  45.0 4.8 %collective-permute-start.6 = (f32[128]{0:T(128)S(1)}, f32[128]{0:T(128)S(1)}, u32[]{:S(2)}, u32[]{:S(2)}) collective-permute-start(f32[128]{0:T(128)S(1)} %collective-permute-done.4), channel_id=1, source_target_pairs={{0,1},{1,4},{4,5},{5,8},{8,9},{9,12},{12,13},{13,0},{2,3},{3,6},{6... | collective-permute-start | bytes 1544 | tf_op jit(solution)/shard_map/ppermute | solution.py:19
  78.2 7.6 %copy-start.1 = (f32[128]{0:T(128)S(1)}, f32[128]{0:T(128)}, u32[]{:S(2)}) copy-start(f32[128]{0:T(128)} %param.9) | copy-start | bytes 1540
  151.7 4.8 %collective-permute-start.7 = (f32[128]{0:T(128)S(1)}, f32[128]{0:T(128)S(1)}, u32[]{:S(2)}, u32[]{:S(2)}) collective-permute-start(f32[128]{0:T(128)S(1)} %get-tuple-element.66), channel_id=1, source_target_pairs={{0,1},{1,4},{4,5},{5,8},{8,9},{9,12},{12,13},{13,0},{2,3},{3,6},{6... | collective-permute-start | bytes 1544 | tf_op jit(solution)/shard_map/ppermute | solution.py:19
  151.8 4.8 %collective-permute-start.8 = (f32[128]{0:T(128)S(1)}, f32[128]{0:T(128)S(1)}, u32[]{:S(2)}, u32[]{:S(2)}) collective-permute-start(f32[128]{0:T(128)S(1)} %get-tuple-element.66), channel_id=1, source_target_pairs={{0,13},{1,0},{4,1},{5,4},{8,5},{9,8},{12,9},{13,12},{2,15},{3,2},{... | collective-permute-start | bytes 1544 | tf_op jit(solution)/shard_map/ppermute | solution.py:24
  156.5 4.8 %collective-permute-start.9 = (f32[128]{0:T(128)S(1)}, f32[128]{0:T(128)S(1)}, u32[]{:S(2)}, u32[]{:S(2)}) collective-permute-start(f32[128]{0:T(128)S(1)} %collective-permute-done.7), channel_id=1, source_target_pairs={{0,1},{1,4},{4,5},{5,8},{8,9},{9,12},{12,13},{13,0},{2,3},{3,6},{6... | collective-permute-start | bytes 1544 | tf_op jit(solution)/shard_map/ppermute | solution.py:19
  156.6 4.8 %collective-permute-start.10 = (f32[128]{0:T(128)S(1)}, f32[128]{0:T(128)S(1)}, u32[]{:S(2)}, u32[]{:S(2)}) collective-permute-start(f32[128]{0:T(128)S(1)} %collective-permute-done.8), channel_id=1, source_target_pairs={{0,13},{1,0},{4,1},{5,4},{8,5},{9,8},{12,9},{13,12},{2,15},{3,2},{... | collective-permute-start | bytes 1544 | tf_op jit(solution)/shard_map/ppermute | solution.py:24
  161.3 4.8 %collective-permute-start.11 = (f32[128]{0:T(128)S(1)}, f32[128]{0:T(128)S(1)}, u32[]{:S(2)}, u32[]{:S(2)}) collective-permute-start(f32[128]{0:T(128)S(1)} %collective-permute-done.9), channel_id=1, source_target_pairs={{0,1},{1,4},{4,5},{5,8},{8,9},{9,12},{12,13},{13,0},{2,3},{3,6},{6... | collective-permute-start | bytes 1544 | tf_op jit(solution)/shard_map/ppermute | solution.py:19
  161.4 5.7 %collective-permute-start.12 = (f32[128]{0:T(128)S(1)}, f32[128]{0:T(128)S(1)}, u32[]{:S(2)}, u32[]{:S(2)}) collective-permute-start(f32[128]{0:T(128)S(1)} %collective-permute-done.10), channel_id=1, source_target_pairs={{0,13},{1,0},{4,1},{5,4},{8,5},{9,8},{12,9},{13,12},{2,15},{3,2},{... | collective-permute-start | bytes 1544 | tf_op jit(solution)/shard_map/ppermute | solution.py:24
  166.1 4.8 %collective-permute-start.13 = (f32[128]{0:T(128)S(1)}, f32[128]{0:T(128)S(1)}, u32[]{:S(2)}, u32[]{:S(2)}) collective-permute-start(f32[128]{0:T(128)S(1)} %collective-permute-done.11), channel_id=1, source_target_pairs={{0,1},{1,4},{4,5},{5,8},{8,9},{9,12},{12,13},{13,0},{2,3},{3,6},{6... | collective-permute-start | bytes 1544 | tf_op jit(solution)/shard_map/ppermute | solution.py:19
Sparse Core Ops, SparseCore 0:
  30.8 27.0 all-gather.2
